TPU v7x, 256 devices: a whole 4x4x8 slice. The times are simulated.
256 devices in a mesh: curve: 128 (over y, z, x_lo, core), chan: 2 (over x_hi).
Axes of the slice: x: 4 (x_hi: 2, x_lo: 2; x = x_hi * 2 + x_lo), y: 4, z: 8, core: 2. Of those that a mesh axis runs over, the one named last changes fastest.
Arguments:
- features: bfloat16 [524288, 256], P('curve', 'chan'), may hold values from -6 to 6
- cotangent: bfloat16 [524288, 256], P('curve', 'chan'), may hold values from -6 to 6
- near_kernel: bfloat16 [4096, 8, 128, 128], P('curve'), may hold values from -0.1875 to 0.1875
- near_index: int32 [4096, 8], P('curve'), may hold values from 0 to 4095, as said below
- near_count: int32 [4096], P('curve'), may hold values from 1 to 8, as said below
- basis_in: bfloat16 [4096, 16, 128], P('curve'), may hold values from -0.09375 to 0.09375
- basis_out: bfloat16 [4096, 128, 16], P('curve'), may hold values from -1.5 to 1.5
- far_kernel: float32 [128, 8, 16, 16], P('curve'), may hold values from -0.5 to 0.5
- far_index: int32 [128, 8], P('curve'), may hold values from 0 to 127, as said below
- channel_mix: float32 [256, 256], replicated, may hold values from -0.375 to 0.375
Outputs:
- layer_out: bfloat16 [524288, 256], P('curve', 'chan')
- feature_grad: bfloat16 [524288, 256], P('curve', 'chan')
Inputs may be any that keep to these rules, and one draw needn't show every extreme that they name: `near_index`: slot 0 of block b holds b; every slot of block b holds a block from b - 32 to b. `near_count`: in every group of 32 blocks one block has all 8 slots live and another block has one. `far_index`: every partner of group g differs from g by 2 or more.
All inputs are finite; a program needn't handle non-finite values.
Results may differ from a plain program's by a relative error of at most 0.006.
Values may be sent and summed in bfloat16 or wider, within the bound.
No kernel may reach another device: no remote copies, remote signals or barrier semaphores. Data moves between devices by JAX's collectives and lax.ppermute only.
A program may use at most 128 MiB of HBM per device.

v0:
```python
import jax
import jax.numpy as jnp
from jax import lax
from jax.sharding import PartitionSpec as P


def shifted(value, axis, steps):
    count = lax.axis_size(axis)
    leading, last = (max(0, -steps), min(count, count - steps))
    return lax.ppermute(value, axis, [(source, source + steps) for source in range(leading, last)])


def split_up(value, dim, count):
    before, after = (value.shape[:dim], value.shape[dim + 1 :])
    return jnp.moveaxis(value.reshape(*before, count, -1, *after), dim, 0)


def sent_and_summed(value, axis, dim):
    blocks = split_up(value, dim, lax.axis_size(axis))
    arrived = lax.all_to_all(blocks, axis, split_axis=0, concat_axis=0, tiled=True)
    return arrived.sum(axis=0)


def body(
    features,
    cotangent,
    near_kernel,
    near_index,
    near_count,
    basis_in,
    basis_out,
    far_kernel,
    far_index,
    channel_mix,
):
    exact = lax.Precision.HIGHEST
    blocks, slots, panels, _ = near_kernel.shape
    width = features.shape[1]
    groups = lax.axis_size("curve")
    position = lax.axis_index("curve")
    chan_pos = lax.axis_index("chan")
    feat_blocks = features.reshape(blocks, panels, width)
    cot_blocks = cotangent.reshape(blocks, panels, width)
    live_slot = lax.iota(jnp.int32, slots)[None, :] < near_count[:, None]
    local_rows = near_index - (position * blocks - blocks)
    coarse = jnp.einsum(
        "brp,bpc->rc", basis_in, feat_blocks, preferred_element_type=jnp.float32
    ).astype(jnp.bfloat16)
    dfar = jnp.einsum("bpr,bpc->rc", basis_out, cot_blocks, preferred_element_type=jnp.float32)
    before = shifted(features, "curve", 1)
    extended = jnp.concatenate([before.reshape(blocks, panels, width), feat_blocks], axis=0)
    picked = extended[local_rows] * live_slot[:, :, None, None].astype(jnp.bfloat16)
    near = jnp.einsum("bspq,bsqc->bpc", near_kernel, picked, preferred_element_type=jnp.float32)
    mix_cols = lax.dynamic_slice_in_dim(channel_mix, chan_pos * width, width, 1)
    far_mats = far_kernel[0]
    partners = far_index[0]
    one_hot = (partners[:, None] == lax.iota(jnp.int32, groups)[None, :]).astype(jnp.float32)
    every = lax.all_gather(coarse[None], "curve", axis=0, tiled=True)
    chosen = jnp.einsum("ag,grc->arc", one_hot, every.astype(jnp.float32), precision=exact)
    partial_coef = jnp.einsum("aqr,arc->qc", far_mats, chosen, precision=exact)
    mix_rows = lax.dynamic_slice_in_dim(channel_mix, chan_pos * width, width, 0)
    term = jnp.dot(partial_coef, mix_rows, precision=exact, preferred_element_type=jnp.float32)
    far_coef = sent_and_summed(term, "chan", 1)
    far_low = far_coef.astype(jnp.bfloat16)
    layer = near + jnp.einsum("bpr,rc->bpc", basis_out, far_low, preferred_element_type=jnp.float32)
    layer_out = layer.astype(jnp.bfloat16).reshape(blocks * panels, width)
    contrib = jnp.einsum(
        "bspq,bpc->bsqc", near_kernel, cot_blocks, preferred_element_type=jnp.float32
    )
    slot_hot = (
        (local_rows[:, :, None] == lax.iota(jnp.int32, 2 * blocks)[None, None, :])
        & live_slot[:, :, None]
    ).astype(jnp.bfloat16)
    contrib_high = contrib.astype(jnp.bfloat16)
    contrib_low = (contrib - contrib_high.astype(jnp.float32)).astype(jnp.bfloat16)
    spread_near = jnp.einsum(
        "bse,bsqc->eqc", slot_hot, contrib_high, preferred_element_type=jnp.float32
    )
    spread_near = spread_near + jnp.einsum(
        "bse,bsqc->eqc", slot_hot, contrib_low, preferred_element_type=jnp.float32
    )
    arrived = shifted(spread_near[:blocks].astype(jnp.bfloat16), "curve", -1).astype(jnp.float32)
    nearback = spread_near[blocks:] + arrived
    unmix_term = jnp.dot(dfar, mix_cols.T, precision=exact, preferred_element_type=jnp.float32)
    dz_share = sent_and_summed(unmix_term, "chan", 1)
    spread = jnp.einsum("aqr,qc->arc", far_mats, dz_share, precision=exact)
    grad_terms = jnp.einsum("ag,arc->grc", one_hot, spread, precision=exact)
    dcoarse = lax.psum_scatter(grad_terms, "curve", scatter_dimension=0, tiled=True)[0]
    dcoarse_low = dcoarse.astype(jnp.bfloat16)
    grad = nearback + jnp.einsum(
        "brp,rc->bpc", basis_in, dcoarse_low, preferred_element_type=jnp.float32
    )
    feature_grad = grad.astype(jnp.bfloat16).reshape(blocks * panels, width)
    return (layer_out, feature_grad)


def solution(mesh):
    return jax.shard_map(
        body,
        mesh=mesh,
        in_specs=(
            P("curve", "chan"),
            P("curve", "chan"),
            P("curve", None, None, None),
            P("curve", None),
            P("curve"),
            P("curve", None, None),
            P("curve", None, None),
            P("curve", None, None, None),
            P("curve", None),
            P(),
        ),
        out_specs=(P("curve", "chan"), P("curve", "chan")),
        check_vma=False,
    )
```

profile of v0, /device:TPU:0, one launch (start us, length us, event | category | flops | bytes accessed | tf_op | source)
XLA Modules:
  0.0 787.8 jit_solution(6620656626656210797)
XLA Ops:
  7.2 0.7 iota_compare_fusion.2
  7.9 0.7 compare_select_fusion
  8.6 7.9 %subtract_convert_fusion = (bf16[32,8,128,128]{3,2,1,0:T(8,128)(2,1)}, bf16[32,8,128,128]{3,2,1,0:T(8,128)(2,1)S(1)}) fusion(bf16[32,8,128,128]{3,2,1,0:T(8,128)(2,1)} %param.12, bf16[32,128,128,1]{2,1,3,0:T(8,128)(2,1)S(1)} %bitcast.89), kind=kOutput, calls=%fused_computation.1 | convolution fusion | flops 1090519040 | bytes 26214400 | tf_op jit(solution)/shard_map/bspq,bpc->bsqc/dot_general | solution.py:67
  16.5 8.4 %fusion = f32[64,128,128,1]{2,0,3,1:T(8,128)S(1)} fusion(bf16[32,8,128,128]{3,2,1,0:T(8,128)(2,1)} %get-tuple-element.2, s32[32,8]{0,1:T(8,128)S(1)} %get-tuple-element.5, pred[32,8]{0,1:T(8,128)(4,1)S(1)} %get-tuple-element.6), kind=kOutput, calls=%fused_computation.2 | convolution fusion | flops 536903680 | bytes 12584192 | tf_op jit(solution)/shard_map/bse,bsqc->eqc/dot_general | solution.py:79
  25.1 5.5 bitcast_add_fusion
  30.5 2.0 copy-done.1
  32.5 1.2 slice.19
  33.7 1.3 collective-permute-start.1
  35.5 0.6 copy.55
  36.1 3.2 all-to-all-start.1
  39.4 4.0 collective-permute-start
  43.7 164.0 %all-gather = bf16[2048,128]{1,0:T(8,128)(2,1)S(1)} all-gather(bf16[16,128]{1,0:T(8,128)(2,1)S(1)} %fusion.14), channel_id=2, replica_groups=mesh['curve'=128,'chan'=2] {'curve'}, dimensions={0}, use_global_device_ids=true | all-gather | bytes 528384 | tf_op jit(solution)/shard_map/all_gather | solution.py:58
  208.0 0.7 fusion.34
  208.7 1.6 copy.34
  211.6 3.9 all-to-all-start
  215.7 1.3 copy.35
  217.0 3.9 all-to-all-done
  220.9 1.8 fusion.29
  222.7 1.7 pad_maximum_fusion
  224.4 8.5 %gather_fusion = bf16[256,128,128]{2,1,0:T(8,128)(2,1)} fusion(bf16[64,128,128]{2,1,0:T(8,128)(2,1)S(1)} %pad_maximum_fusion, s32[1024]{0:T(1024)S(1)} %pad_clamp_fusion), kind=kCustom, calls=%fused_computation | custom fusion | bytes 16778240 | tf_op jit(solution)/shard_map/gather | solution.py:52
  233.0 9.9 %fusion.11 = bf16[32,128,128]{2,1,0:T(8,128)(2,1)} fusion(f32[128,32,128]{0,2,1:T(8,128)} %fusion.29, bf16[32,8,128,128]{3,2,1,0:T(8,128)(2,1)} %param.12, bf16[32,8,128,128]{3,2,1,0:T(8,128)(2,1)} %bitcast.91, bf16[32,8]{1,0:T(8,128)(2,1)S(1)} %copy.25), kind=kOutput, calls=%fused_computation.16 | convolution fusion | flops 1091567616 | bytes 19923456 | tf_op jit(solution)/shard_map/bspq,bsqc->bpc/dot_general | solution.py:53
  242.8 534.3 %reduce-scatter.2.cloned.1.call-done = f32[1,16,128]{2,1,0:T(8,128)} async-done(((f32[128,16,128]{2,1,0:T(8,128)}), f32[1,16,128]{2,1,0:T(8,128)}) %reduce-scatter.2.cloned.1.call-update) | async-done | bytes 8208 | tf_op jit(solution)/shard_map/reduce_scatter | solution.py:88
  777.2 2.4 fusion.10
  779.6 1.4 copy.36
  (37 shorter events, 2.6 us)
Async XLA Ops:
  7.2 1.5 copy-start
  25.0 10.0 %copy-start.5 = (bf16[32,128,16]{1,2,0:T(8,128)(2,1)S(1)}, bf16[32,128,16]{1,2,0:T(8,128)(2,1)}, u32[]{:S(2)}) copy-start(bf16[32,128,16]{1,2,0:T(8,128)(2,1)} %param.16) | copy-start | bytes 393220
  25.0 10.3 %copy-start.6 = (f32[256,256]{1,0:T(8,128)S(1)}, f32[256,256]{1,0:T(8,128)}, u32[]{:S(2)}) copy-start(f32[256,256]{1,0:T(8,128)} %param.19) | copy-start | bytes 786436
  25.0 14.4 %copy-start.2 = (bf16[4096,128]{1,0:T(8,128)(2,1)S(1)}, bf16[4096,128]{1,0:T(8,128)(2,1)}, u32[]{:S(2)}) copy-start(bf16[4096,128]{1,0:T(8,128)(2,1)} %param.10) | copy-start | bytes 3145732
  25.0 18.4 %copy-start.4 = (bf16[32,16,128]{2,1,0:T(8,128)(2,1)S(1)}, bf16[32,16,128]{2,1,0:T(8,128)(2,1)}, u32[]{:S(2)}) copy-start(bf16[32,16,128]{2,1,0:T(8,128)(2,1)} %param.15) | copy-start | bytes 393220
  25.0 182.6 %copy-start.7 = (f32[1,8,16,16]{3,2,1,0:T(8,128)S(1)}, f32[1,8,16,16]{3,2,1,0:T(8,128)}, u32[]{:S(2)}) copy-start(f32[1,8,16,16]{3,2,1,0:T(8,128)} %param.17) | copy-start | bytes 24580
  25.0 182.9 %copy-start.8 = (s32[1,8]{1,0:T(1,128)S(1)}, s32[1,8]{1,0:T(1,128)}, u32[]{:S(2)}) copy-start(s32[1,8]{1,0:T(1,128)} %param.18) | copy-start | bytes 100
  30.5 2.0 copy-start.1
  33.7 209.1 %collective-permute-start.1 = (bf16[32,128,128]{2,0,1:T(8,128)(2,1)}, bf16[32,128,128]{2,0,1:T(8,128)(2,1)}, u32[]{:S(2)}, u32[]{:S(2)}) collective-permute-start(bf16[32,128,128]{2,0,1:T(8,128)(2,1)} %slice.19), channel_id=1, source_target_pairs={{2,0},{4,2},{6,4},{8,6},{10,8},{12,10},{14,12},{16,14},{18,16},{20... | collective-permute-start | bytes 3145736 | tf_op jit(solution)/shard_map/ppermute | solution.py:10
  36.1 171.6 %all-to-all-start.1 = ((f32[2,16,128]{2,1,0:T(8,128)}), f32[2,16,128]{2,1,0:T(8,128)S(1)}, u32[]{:S(2)}, u32[]{:S(2)}) async-start(f32[2,16,128]{2,1,0:T(8,128)} %bitcast.86), calls=%async_computation.1 | async-start | bytes 32768 | tf_op jit(solution)/shard_map/all_to_all | solution.py:20
  39.4 737.8 %reduce-scatter.2.cloned.1.call-start = ((), (), s32[]{:S(2)}) async-start(), calls=%async_computation.3 | async-start | bytes 1056768 | tf_op jit(solution)/shard_map/reduce_scatter | solution.py:88
  39.4 183.3 %collective-permute-start = (bf16[4096,128]{1,0:T(8,128)(2,1)S(1)}, bf16[4096,128]{1,0:T(8,128)(2,1)}, u32[]{:S(2)}, u32[]{:S(2)}) collective-permute-start(bf16[4096,128]{1,0:T(8,128)(2,1)S(1)} %copy-done.2), channel_id=1, source_target_pairs={{0,2},{2,4},{4,6},{6,8},{8,10},{10,12},{12,14},{14,16},{16,18},{18... | collective-permute-start | bytes 3145736 | tf_op jit(solution)/shard_map/ppermute | solution.py:10
  211.6 9.3 %all-to-all-start = ((f32[2,16,128]{2,1,0:T(8,128)}), f32[2,16,128]{2,1,0:T(8,128)S(1)}, u32[]{:S(2)}, u32[]{:S(2)}) async-start(f32[2,16,128]{2,1,0:T(8,128)} %bitcast.88), calls=%async_computation | async-start | bytes 32768 | tf_op jit(solution)/shard_map/all_to_all | solution.py:20
  233.0 544.2 %copy-start.3 = (bf16[32,16,128]{0,1,2:T(8,128)(2,1)S(1)}, bf16[32,16,128]{0,1,2:T(8,128)(2,1)}, u32[]{:S(2)}) copy-start(bf16[32,16,128]{0,1,2:T(8,128)(2,1)} %copy.35) | copy-start | bytes 393220
Sparse Core Ops, SparseCore 0:
  210.4 566.7 reduce-scatter.1
where the time goes:
time: 788 us
  waiting for transfers between devices  538 us (68%)
  blocking collectives  164 us (21%)
  matrix products  38.2 us (5%)
  local copies, waits for them, and re-layouts  17.6 us (2%)
  between operations  14.2 us (2%)
  starting transfers between devices  12.5 us (2%)
    reduce_scatter x1, waiting for transfers between devices, body(): lax.psum_scatter(grad_terms, 'curve', scatter_dimension=0, tiled=True)[0]  534 us
    all_gather x1, blocking collectives, body(): every = lax.all_gather(coarse[None], 'curve', axis=0, tiled=True)  164 us
  transfers between devices with their start and end apart: 5, of which 2 were waited for; matrix products, arithmetic and copies ran while one was open for 4% of the time, Pallas kernels for 0%

commit v1 on v0

--- a/solution.py
+++ b/solution.py
@@ -55,7 +55,9 @@
     far_mats = far_kernel[0]
     partners = far_index[0]
     one_hot = (partners[:, None] == lax.iota(jnp.int32, groups)[None, :]).astype(jnp.float32)
-    every = lax.all_gather(coarse[None], "curve", axis=0, tiled=True)
+    block = coarse[None]
+    sent = jnp.stack([block] * lax.axis_size("curve"))
+    every = jnp.concatenate(lax.all_to_all(sent, "curve", 0, 0), axis=0)
     chosen = jnp.einsum("ag,grc->arc", one_hot, every.astype(jnp.float32), precision=exact)
     partial_coef = jnp.einsum("aqr,arc->qc", far_mats, chosen, precision=exact)
     mix_rows = lax.dynamic_slice_in_dim(channel_mix, chan_pos * width, width, 0)

time: 788 us -> 654 us (0.83)
  blocking collectives: 164 us -> 0 us
  starting transfers between devices: 12.5 us -> 25.7 us
  waiting for transfers between devices: 538 us -> 547 us
    all_gather x1 -> x0, blocking collectives: 164 us -> none  [body(): every = lax.all_gather(coarse[None], 'curve', axis=0, tiled=True)]
    all_to_all x0 -> x1, starting transfers between devices: none -> 14.8 us  [body(): every = jnp.concatenate(lax.all_to_all(sent, 'curve', 0, 0), axis=0)]
    reduce_scatter x1, waiting for transfers between devices: 534 us -> 547 us  [body(): lax.psum_scatter(grad_terms, 'curve', scatter_dimension=0, tiled=True)[0]]
  transfers between devices with their start and end apart: 5 -> 6, of which waited for: 2 -> 2; matrix products, arithmetic and copies ran while one was open for 4% -> 8% of each run, Pallas kernels for 0% -> 0%
where the time goes in v1:
time: 654 us; the launch traced here: 652 us
  waiting for transfers between devices  547 us (84%)
  matrix products  41.2 us (6%)
  starting transfers between devices  25.7 us (4%)
  local copies, waits for them, and re-layouts  20.6 us (3%)
  between operations  14.2 us (2%)
    reduce_scatter x1, waiting for transfers between devices, body(): lax.psum_scatter(grad_terms, 'curve', scatter_dimension=0, tiled=True)[0]  547 us
    all_to_all x1, starting transfers between devices, body(): every = jnp.concatenate(lax.all_to_all(sent, 'curve', 0, 0), axis=0)  14.8 us
  transfers between devices with their start and end apart: 6, of which 2 were waited for; matrix products, arithmetic and copies ran while one was open for 8% of the time, Pallas kernels for 0%

profile of v1, /device:TPU:0, one launch (start us, length us, event | category | flops | bytes accessed | tf_op | source)
XLA Modules:
  0.0 652.1 jit_solution(13036402640979762524)
XLA Ops:
  7.2 1.2 copy-done
  8.4 1.1 convolution_bitcast_fusion.3
  9.5 1.1 convolution_bitcast_fusion.1
  11.3 3.2 all-to-all-start.2
  14.5 1.4 collective-permute-start
  16.6 0.7 compare_select_fusion
  17.3 7.9 %subtract_convert_fusion = (bf16[32,8,128,128]{3,2,1,0:T(8,128)(2,1)S(1)}, bf16[32,8,128,128]{3,2,1,0:T(8,128)(2,1)}) fusion(bf16[32,8,128,128]{3,2,1,0:T(8,128)(2,1)} %param.12, bf16[32,128,128,1]{2,1,3,0:T(8,128)(2,1)S(1)} %bitcast.91), kind=kOutput, calls=%fused_computation.1 | convolution fusion | flops 1090519040 | bytes 26214400 | tf_op jit(solution)/shard_map/bspq,bpc->bsqc/dot_general | solution.py:69
  25.2 7.0 %fusion = f32[64,128,128,1]{2,0,3,1:T(8,128)} fusion(bf16[32,8,128,128]{3,2,1,0:T(8,128)(2,1)S(1)} %get-tuple-element.2, s32[32,8]{0,1:T(8,128)S(1)} %get-tuple-element.5, pred[32,8]{0,1:T(8,128)(4,1)S(1)} %get-tuple-element.6), kind=kOutput, calls=%fused_computation.2 | convolution fusion | flops 536903680 | bytes 12584192 | tf_op jit(solution)/shard_map/bse,bsqc->eqc/dot_general | solution.py:81
  32.5 0.9 stack.3
  33.4 14.8 %all-to-all-start = ((bf16[128,1,16,128]{3,2,1,0:T(8,128)(2,1)}), bf16[128,1,16,128]{3,2,1,0:T(8,128)(2,1)S(1)}, u32[]{:S(2)}, u32[]{:S(2)}) async-start(bf16[128,1,16,128]{3,2,1,0:T(8,128)(2,1)} %stack.3), calls=%async_computation | async-start | bytes 1048576 | tf_op jit(solution)/shard_map/all_to_all | solution.py:60
  48.5 9.9 %bitcast_add_fusion = f32[64,128,128]{2,0,1:T(8,128)S(1)} fusion(f32[64,128,128,1]{2,0,3,1:T(8,128)} %fusion, bf16[32,8,128,128]{3,2,1,0:T(8,128)(2,1)} %get-tuple-element.3, s32[32,8]{0,1:T(8,128)S(1)} %get-tuple-element.5, pred[32,8]{0,1:T(8,128)(4,1)S(1)} %get-tuple-element.6), kind=kOutput, calls=%fused_computation.8 | convolution fusion | flops 537952256 | bytes 16778496 | tf_op jit(solution)/shard_map/bse,bsqc->eqc/dot_general | solution.py:78
  58.4 2.0 copy-done.1
  60.4 1.2 slice.19
  61.6 1.3 collective-permute-start.1
  64.1 1.6 copy.46
  65.7 1.3 copy.47
  68.5 4.8 all-to-all-start.1
  73.3 1.0 copy-done.4
  74.3 1.7 pad_maximum_fusion
  76.0 8.5 %gather_fusion = bf16[256,128,128]{2,1,0:T(8,128)(2,1)} fusion(bf16[64,128,128]{2,1,0:T(8,128)(2,1)S(1)} %pad_maximum_fusion, s32[1024]{0:T(1024)S(1)} %pad_clamp_fusion), kind=kCustom, calls=%fused_computation | custom fusion | bytes 16778240 | tf_op jit(solution)/shard_map/gather | solution.py:52
  85.1 9.3 %fusion.11 = bf16[32,128,128]{2,1,0:T(8,128)(2,1)} fusion(f32[128,32,128]{0,2,1:T(8,128)S(1)} %fusion.30, bf16[32,8,128,128]{3,2,1,0:T(8,128)(2,1)} %param.12, bf16[32,8,128,128]{3,2,1,0:T(8,128)(2,1)} %bitcast.93, bf16[32,8]{1,0:T(8,128)(2,1)S(1)} %copy.37), kind=kOutput, calls=%fused_computation.16 | convolution fusion | flops 1091567616 | bytes 19923456 | tf_op jit(solution)/shard_map/bspq,bsqc->bpc/dot_general | solution.py:53
  94.4 547.0 %reduce-scatter.2.cloned.1.call-done = f32[1,16,128]{2,1,0:T(8,128)} async-done(((f32[128,16,128]{2,1,0:T(8,128)}), f32[1,16,128]{2,1,0:T(8,128)}) %reduce-scatter.2.cloned.1.call-update) | async-done | bytes 8208 | tf_op jit(solution)/shard_map/reduce_scatter | solution.py:90
  641.5 2.4 fusion.10
  643.9 1.4 copy.48
  (41 shorter events, 5.0 us)
Async XLA Ops:
  7.2 1.2 copy-start
  11.3 21.2 %all-to-all-start.2 = ((f32[2,16,128]{2,1,0:T(8,128)}), f32[2,16,128]{2,1,0:T(8,128)S(1)}, u32[]{:S(2)}, u32[]{:S(2)}) async-start(f32[2,16,128]{2,1,0:T(8,128)} %bitcast.88), calls=%async_computation.2 | async-start | bytes 32768 | tf_op jit(solution)/shard_map/all_to_all | solution.py:20
  14.5 58.8 %collective-permute-start = (bf16[4096,128]{1,0:T(8,128)(2,1)}, bf16[4096,128]{1,0:T(8,128)(2,1)S(1)}, u32[]{:S(2)}, u32[]{:S(2)}) collective-permute-start(bf16[4096,128]{1,0:T(8,128)(2,1)} %param.10), channel_id=1, source_target_pairs={{0,2},{2,4},{4,6},{6,8},{8,10},{10,12},{12,14},{14,16},{16,18},{18... | collective-permute-start | bytes 3145736 | tf_op jit(solution)/shard_map/ppermute | solution.py:10
  25.2 7.1 %copy-start.2 = (bf16[4096,128]{1,0:T(8,128)(2,1)S(1)}, bf16[4096,128]{1,0:T(8,128)(2,1)}, u32[]{:S(2)}) copy-start(bf16[4096,128]{1,0:T(8,128)(2,1)} %param.10) | copy-start | bytes 3145732
  25.2 7.1 %copy-start.5 = (bf16[32,16,128]{2,1,0:T(8,128)(2,1)S(1)}, bf16[32,16,128]{2,1,0:T(8,128)(2,1)}, u32[]{:S(2)}) copy-start(bf16[32,16,128]{2,1,0:T(8,128)(2,1)} %param.15) | copy-start | bytes 393220
  33.4 33.9 %all-to-all-start = ((bf16[128,1,16,128]{3,2,1,0:T(8,128)(2,1)}), bf16[128,1,16,128]{3,2,1,0:T(8,128)(2,1)S(1)}, u32[]{:S(2)}, u32[]{:S(2)}) async-start(bf16[128,1,16,128]{3,2,1,0:T(8,128)(2,1)} %stack.3), calls=%async_computation | async-start | bytes 1048576 | tf_op jit(solution)/shard_map/all_to_all | solution.py:60
  48.2 593.2 %reduce-scatter.2.cloned.1.call-start = ((), (), s32[]{:S(2)}) async-start(), calls=%async_computation.4 | async-start | bytes 1056768 | tf_op jit(solution)/shard_map/reduce_scatter | solution.py:90
  48.4 14.5 %copy-start.8 = (f32[1,8,16,16]{3,2,1,0:T(8,128)S(1)}, f32[1,8,16,16]{3,2,1,0:T(8,128)}, u32[]{:S(2)}) copy-start(f32[1,8,16,16]{3,2,1,0:T(8,128)} %param.17) | copy-start | bytes 24580
  48.5 14.9 %copy-start.9 = (s32[1,8]{1,0:T(1,128)S(1)}, s32[1,8]{1,0:T(1,128)}, u32[]{:S(2)}) copy-start(s32[1,8]{1,0:T(1,128)} %param.18) | copy-start | bytes 100
  48.5 19.2 %copy-start.7 = (f32[256,256]{1,0:T(8,128)S(1)}, f32[256,256]{1,0:T(8,128)}, u32[]{:S(2)}) copy-start(f32[256,256]{1,0:T(8,128)} %param.19) | copy-start | bytes 786436
  58.4 2.0 copy-start.1
  61.6 32.8 %collective-permute-start.1 = (bf16[32,128,128]{2,0,1:T(8,128)(2,1)}, bf16[32,128,128]{2,0,1:T(8,128)(2,1)}, u32[]{:S(2)}, u32[]{:S(2)}) collective-permute-start(bf16[32,128,128]{2,0,1:T(8,128)(2,1)} %slice.19), channel_id=1, source_target_pairs={{2,0},{4,2},{6,4},{8,6},{10,8},{12,10},{14,12},{16,14},{18,16},{20... | collective-permute-start | bytes 3145736 | tf_op jit(solution)/shard_map/ppermute | solution.py:10
  68.5 16.0 %all-to-all-start.1 = ((f32[2,16,128]{2,1,0:T(8,128)}), f32[2,16,128]{2,1,0:T(8,128)S(1)}, u32[]{:S(2)}, u32[]{:S(2)}) async-start(f32[2,16,128]{2,1,0:T(8,128)} %bitcast.90), calls=%async_computation.1 | async-start | bytes 32768 | tf_op jit(solution)/shard_map/all_to_all | solution.py:20
  73.3 1.0 copy-start.4
  76.0 8.5 %copy-start.6 = (bf16[32,128,16]{1,2,0:T(8,128)(2,1)S(1)}, bf16[32,128,16]{1,2,0:T(8,128)(2,1)}, u32[]{:S(2)}) copy-start(bf16[32,128,16]{1,2,0:T(8,128)(2,1)} %param.16) | copy-start | bytes 393220
  85.1 556.4 %copy-start.3 = (bf16[32,16,128]{0,1,2:T(8,128)(2,1)S(1)}, bf16[32,16,128]{0,1,2:T(8,128)(2,1)}, u32[]{:S(2)}) copy-start(bf16[32,16,128]{0,1,2:T(8,128)(2,1)} %copy.47) | copy-start | bytes 393220
Sparse Core Ops, SparseCore 0:
  65.8 575.5 reduce-scatter.1
